TPU v7x, 512 devices: a whole 4x4x16 slice. The times are simulated.
512 devices in a mesh: dp: 16 (over z_lo, y), pipe: 4 (over x), tensor: 8 (over z_hi, core).
Axes of the slice: x: 4, y: 4, z: 16 (z_hi: 4, z_lo: 4; z = z_hi * 4 + z_lo), core: 2. Of those that a mesh axis runs over, the one named last changes fastest.
Arguments:
- section_out: bfloat16 [4, 2048, 12288], P('pipe', 'dp', 'tensor'), may hold values from -6 to 6
- embedded: bfloat16 [2048, 12288], P('dp', 'tensor'), may hold values from -6 to 6
- cot_norm: bfloat16 [4, 2048, 12288], P('pipe', 'dp', 'tensor'), may hold values from -3 to 3
- cot_res: bfloat16 [4, 2048, 12288], P('pipe', 'dp', 'tensor'), may hold values from -3 to 3
- gain: bfloat16 [4, 64, 12288], P('pipe', None, 'tensor'), may hold values from 0.25 to 1.75
- bias: bfloat16 [4, 64, 12288], P('pipe', None, 'tensor'), may hold values from -1.5 to 1.5
- lang_ids: int32 [2048], P('dp'), may hold values from 0 to 63
- mb_order: int32 [16, 4], P('dp'), may hold values from 0 to 3, each once within a row
Outputs:
- normed_out: bfloat16 [4, 2048, 12288], P('pipe', 'dp', 'tensor')
- returned_grad: bfloat16 [4, 2048, 12288], P('pipe', 'dp', 'tensor')
- gain_grad: float32 [4, 64, 12288], P('pipe', None, 'tensor')
- bias_grad: float32 [4, 64, 12288], P('pipe', None, 'tensor')
Inputs may be any that keep to these rules, and one draw needn't show every extreme that they name: `lang_ids`: a language id for every token. `mb_order`: each replica's row is a permutation of the 4 micro-batches.
All inputs are finite; a program needn't handle non-finite values.
Results may differ from a plain program's by a relative error of at most 0.0004.
Values may be sent and summed in bfloat16 or wider, within the bound.
No kernel may reach another device: no remote copies, remote signals or barrier semaphores. Data moves between devices by JAX's collectives and lax.ppermute only.
A program may use at most 64 MiB of HBM per device.

v0:
```python
import jax
import jax.numpy as jnp
from jax import lax
from jax.sharding import PartitionSpec as P

D = 12288
MB = 4
eps = 1e-05


def shifted(value, axis, steps):
    count = lax.axis_size(axis)
    leading, last = (max(0, -steps), min(count, count - steps))
    return lax.ppermute(value, axis, [(source, source + steps) for source in range(leading, last)])


def passed_along(array, axis, by):
    length = lax.axis_size(axis)
    return lax.ppermute(array, axis, [(i, (i + by) % length) for i in range(length)])


def reorder(values, order):
    shaped = values.reshape((MB, -1) + values.shape[1:])
    return jnp.take(shaped, order, axis=0).reshape(values.shape)


def invert(order):
    slots = jnp.arange(MB, dtype=jnp.int32)
    hits = (order[:, None] == slots[None, :]).astype(jnp.int32)
    return jnp.sum(slots[:, None] * hits, axis=0)


def local(section_out, embedded, cot_norm, cot_res, gain, bias, lang_ids, mb_order):
    local_width = embedded.shape[1]
    langs = gain.shape[1]
    received = shifted(section_out, "pipe", 1)
    is_first = lax.axis_index("pipe") == 0
    inputs = jnp.where(is_first, embedded, received[0]).astype(jnp.float32)
    order = mb_order[0]
    inverse = invert(order)
    cot_fwd = reorder(cot_norm[0], inverse).astype(jnp.float32)
    pass_fwd = reorder(cot_res[0], inverse).astype(jnp.float32)
    matches = lang_ids[:, None] == jnp.arange(langs, dtype=jnp.int32)[None, :]
    selector = matches.astype(jnp.bfloat16)
    gain_rows = jnp.dot(selector, gain[0], preferred_element_type=jnp.float32)
    bias_rows = jnp.dot(selector, bias[0], preferred_element_type=jnp.float32)
    scaled_cot = cot_fwd * gain_rows
    moment_one, moment_two = lax.psum(
        (jnp.sum(inputs, axis=1), jnp.sum(inputs * inputs, axis=1)), "tensor"
    )
    center = moment_one[:, None] / D
    spread = moment_two[:, None] / D - center * center
    inv_scale = lax.rsqrt(spread + eps)
    normalized = (inputs - center) * inv_scale
    cot_total, cross_total = lax.psum(
        (jnp.sum(scaled_cot, axis=1), jnp.sum(scaled_cot * normalized, axis=1)), "tensor"
    )
    mean_cot = cot_total[:, None] / D
    mean_cross = cross_total[:, None] / D
    normed = (normalized * gain_rows + bias_rows).astype(jnp.bfloat16)
    input_grad = (pass_fwd + inv_scale * (scaled_cot - mean_cot - normalized * mean_cross)).astype(
        jnp.bfloat16
    )
    sent_back = reorder(input_grad, order)
    returned = passed_along(sent_back[None], "pipe", -1)
    products = jnp.concatenate([cot_fwd * normalized, cot_fwd], axis=1)
    local_sums = jnp.dot(
        matches.astype(jnp.float32).T,
        products,
        precision=lax.Precision.HIGHEST,
        preferred_element_type=jnp.float32,
    )
    summed = lax.psum(local_sums, "dp")
    return (normed[None], returned, summed[:, :local_width][None], summed[:, local_width:][None])


def solution(mesh):
    return jax.shard_map(
        local,
        mesh=mesh,
        in_specs=(
            P("pipe", "dp", "tensor"),
            P("dp", "tensor"),
            P("pipe", "dp", "tensor"),
            P("pipe", "dp", "tensor"),
            P("pipe", None, "tensor"),
            P("pipe", None, "tensor"),
            P("dp"),
            P("dp", None),
        ),
        out_specs=(
            P("pipe", "dp", "tensor"),
            P("pipe", "dp", "tensor"),
            P("pipe", None, "tensor"),
            P("pipe", None, "tensor"),
        ),
        check_vma=False,
    )
```

profile of v0, /device:TPU:2, one launch (start us, length us, event | category | flops | bytes accessed | tf_op | source)
XLA Modules:
  0.0 227.5 jit_solution(1984460876628142965)
XLA Ops:
  7.2 0.0 copy-start
  7.2 0.0 copy-start.2
  7.2 0.0 all-reduce.4.cloned.1.call-start
  7.2 3.5 %collective-permute-start = (bf16[1,128,1536]{2,1,0:T(8,128)(2,1)}, bf16[1,128,1536]{2,1,0:T(8,128)(2,1)S(1)}, u32[]{:S(2)}, u32[]{:S(2)}) collective-permute-start(bf16[1,128,1536]{2,1,0:T(8,128)(2,1)} %param.10), channel_id=1, source_target_pairs={{0,8},{8,16},{16,24},{1,9},{9,17},{17,25},{2,10},{10,18},{18,26},{... | collective-permute-start | bytes 1179656 | tf_op jit(solution)/shard_map/ppermute | solution.py:14
  10.8 0.7 select_reduce_fusion
  11.5 0.7 compare_select_fusion
  12.2 0.7 compare_and_fusion
  12.9 0.0 copy-done
  12.9 0.6 gather_fusion
  13.5 0.0 copy-done.2
  13.5 0.6 gather_fusion.1
  14.1 0.1 broadcast_select_fusion.1
  14.2 0.0 copy-start.1
  14.2 0.1 bitcast_convert_fusion
  14.3 0.0 copy-start.3
  14.3 0.0 copy-start.5
  14.3 6.2 %collective-permute-done = bf16[1,128,1536]{2,1,0:T(8,128)(2,1)S(1)} collective-permute-done((bf16[1,128,1536]{2,1,0:T(8,128)(2,1)}, bf16[1,128,1536]{2,1,0:T(8,128)(2,1)S(1)}, u32[]{:S(2)}, u32[]{:S(2)}) %collective-permute-start) | collective-permute-done | bytes 393248 | tf_op jit(solution)/shard_map/ppermute | solution.py:14
  20.5 0.0 copy-done.1
  20.5 0.2 convert_reduce_fusion
  20.8 27.0 %all-reduce.1 = (f32[128]{0:T(128)S(1)}, f32[128]{0:T(128)S(1)}) all-reduce(f32[128]{0:T(128)S(1)} %get-tuple-element.8, f32[128]{0:T(128)S(1)} %get-tuple-element.7), channel_id=1, replica_groups=mesh['dp'=16,'pipe'=4,'tensor'=8] {'tensor'}, use_global_device_ids=true, to_apply=%region_3.4 | all-reduce | flops 256 | bytes 2048 | tf_op jit(solution)/shard_map/psum | solution.py:48
  47.8 0.0 copy-done.3
  47.8 0.0 copy-done.5
  47.8 0.5 fusion.17
  48.3 1.7 fusion.2
  50.0 0.0 all-reduce.4.cloned.1.call-update
  50.0 18.8 %all-reduce = (f32[128]{0:T(128)S(1)}, f32[128]{0:T(128)S(1)}) all-reduce(f32[128]{0:T(128)S(1)} %get-tuple-element.6, f32[128]{0:T(128)S(1)} %get-tuple-element.5), channel_id=1, replica_groups=mesh['dp'=16,'pipe'=4,'tensor'=8] {'tensor'}, use_global_device_ids=true, to_apply=%region_8.10 | all-reduce | flops 256 | bytes 2048 | tf_op jit(solution)/shard_map/psum | solution.py:55
  68.8 0.4 fusion.15
  69.1 0.0 copy-start.4
  69.1 0.6 gather_fusion.2
  69.7 0.1 broadcast_select_fusion
  69.8 1.9 collective-permute-start.1
  71.8 0.0 copy-done.4
  71.8 1.1 fusion.1
  72.8 8.8 %collective-permute-done.1 = bf16[1,128,1536]{2,1,0:T(8,128)(2,1)S(1)} collective-permute-done((bf16[1,128,1536]{2,1,0:T(8,128)(2,1)S(1)}, bf16[1,128,1536]{2,1,0:T(8,128)(2,1)S(1)}, u32[]{:S(2)}, u32[]{:S(2)}) %collective-permute-start.1) | collective-permute-done | bytes 393248 | tf_op jit(solution)/shard_map/ppermute | solution.py:19
  81.7 136.2 %all-reduce.4.cloned.1.call-done = f32[64,3072]{1,0:T(8,128)} async-done(((f32[64,3072]{1,0:T(8,128)}), f32[64,3072]{1,0:T(8,128)}) %all-reduce.4.cloned.1.call-update) | async-done | bytes 786448 | tf_op jit(solution)/shard_map/psum | solution.py:73
  217.9 2.0 slice_bitcast_fusion
  220.0 0.7 copy.14
  (6 shorter events, 0.0 us)
Async XLA Ops:
  7.2 5.7 %copy-start = (bf16[1,128,1536]{2,1,0:T(8,128)(2,1)S(1)}, bf16[1,128,1536]{2,1,0:T(8,128)(2,1)}, u32[]{:S(2)}) copy-start(bf16[1,128,1536]{2,1,0:T(8,128)(2,1)} %param.13) | copy-start | bytes 1179652
  7.2 6.3 %copy-start.2 = (bf16[1,128,1536]{2,1,0:T(8,128)(2,1)S(1)}, bf16[1,128,1536]{2,1,0:T(8,128)(2,1)}, u32[]{:S(2)}) copy-start(bf16[1,128,1536]{2,1,0:T(8,128)(2,1)} %param.12) | copy-start | bytes 1179652
  7.2 210.7 %all-reduce.4.cloned.1.call-start = ((), (), s32[]{:S(2)}) async-start(), calls=%async_computation | async-start | bytes 1572864 | tf_op jit(solution)/shard_map/psum | solution.py:73
  7.2 13.3 %collective-permute-start = (bf16[1,128,1536]{2,1,0:T(8,128)(2,1)}, bf16[1,128,1536]{2,1,0:T(8,128)(2,1)S(1)}, u32[]{:S(2)}, u32[]{:S(2)}) collective-permute-start(bf16[1,128,1536]{2,1,0:T(8,128)(2,1)} %param.10), channel_id=1, source_target_pairs={{0,8},{8,16},{16,24},{1,9},{9,17},{17,25},{2,10},{10,18},{18,26},{... | collective-permute-start | bytes 1179656 | tf_op jit(solution)/shard_map/ppermute | solution.py:14
  14.2 6.3 %copy-start.1 = (bf16[128,1536]{1,0:T(8,128)(2,1)S(1)}, bf16[128,1536]{1,0:T(8,128)(2,1)}, u32[]{:S(2)}) copy-start(bf16[128,1536]{1,0:T(8,128)(2,1)} %param.11) | copy-start | bytes 1179652
  14.3 33.5 %copy-start.3 = (bf16[1,64,1536]{2,1,0:T(8,128)(2,1)S(1)}, bf16[1,64,1536]{2,1,0:T(8,128)(2,1)}, u32[]{:S(2)}) copy-start(bf16[1,64,1536]{2,1,0:T(8,128)(2,1)} %param.14) | copy-start | bytes 589828
  14.3 33.5 %copy-start.5 = (s32[128]{0:T(128)S(1)}, s32[128]{0:T(128)}, u32[]{:S(2)}) copy-start(s32[128]{0:T(128)} %param.16) | copy-start | bytes 1540
  69.1 2.6 %copy-start.4 = (bf16[1,64,1536]{2,1,0:T(8,128)(2,1)S(1)}, bf16[1,64,1536]{2,1,0:T(8,128)(2,1)}, u32[]{:S(2)}) copy-start(bf16[1,64,1536]{2,1,0:T(8,128)(2,1)} %param.15) | copy-start | bytes 589828
  69.8 11.8 %collective-permute-start.1 = (bf16[1,128,1536]{2,1,0:T(8,128)(2,1)S(1)}, bf16[1,128,1536]{2,1,0:T(8,128)(2,1)S(1)}, u32[]{:S(2)}, u32[]{:S(2)}) collective-permute-start(bf16[1,128,1536]{2,1,0:T(8,128)(2,1)S(1)} %bitcast.42), channel_id=1, source_target_pairs={{0,24},{8,0},{16,8},{24,16},{1,25},{9,1},{17,9},{25,17},{2,26},{10... | collective-permute-start | bytes 1179656 | tf_op jit(solution)/shard_map/ppermute | solution.py:19
Sparse Core Ops, SparseCore 0:
  50.1 167.7 all-reduce.3
where the time goes:
time: 228 us
  waiting for transfers between devices  151 us (66%)
  blocking collectives  45.8 us (20%)
  between operations  14.2 us (6%)
  starting transfers between devices  5.49 us (2%)
  local copies, waits for them, and re-layouts  4.55 us (2%)
  matrix products  3.23 us (1%)
  other arithmetic  3.06 us (1%)
    psum x1, waiting for transfers between devices, local(): summed = lax.psum(local_sums, 'dp')  136 us
    psum x1, blocking collectives, local(): lax.psum((jnp.sum(inputs, axis=1), jnp.sum(inputs * inputs, axis=1)), 'te...  27 us
    psum x1, blocking collectives, local(): lax.psum((jnp.sum(scaled_cot, axis=1), jnp.sum(scaled_cot * normalized, a...  18.8 us
    ppermute x1, waiting for transfers between devices, passed_along(): lax.ppermute(array, axis, [(i, (i + by) % length) for i in range(length)])  8.85 us
    ppermute x1, waiting for transfers between devices, shifted(): lax.ppermute(value, axis, [(source, source + steps) for source in range(l...  6.17 us
  transfers between devices with their start and end apart: 3, of which 3 were waited for; matrix products, arithmetic and copies ran while one was open for 2% of the time, Pallas kernels for 0%

commit v1 on v0

--- a/solution.py
+++ b/solution.py
@@ -70,7 +70,8 @@
         precision=lax.Precision.HIGHEST,
         preferred_element_type=jnp.float32,
     )
-    summed = lax.psum(local_sums, "dp")
+    parts = lax.all_gather(local_sums, "dp")
+    summed = jnp.sum(parts, axis=0)
     return (normed[None], returned, summed[:, :local_width][None], summed[:, local_width:][None])
 
 

time: 228 us -> 211 us (0.925)
  the two profiles are of different devices: /device:TPU:2 before, /device:TPU:1 now
where the time goes in v1:
time: 211 us
  waiting for transfers between devices  122 us (58%)
  blocking collectives  49 us (23%)
  between operations  14.2 us (7%)
  starting transfers between devices  10.2 us (5%)
  other arithmetic  8.14 us (4%)
  local copies, waits for them, and re-layouts  4.43 us (2%)
  matrix products  3.24 us (2%)
    all_gather x1, waiting for transfers between devices, local(): parts = lax.all_gather(local_sums, 'dp')  115 us
    psum x1, blocking collectives, local(): lax.psum((jnp.sum(inputs, axis=1), jnp.sum(inputs * inputs, axis=1)), 'te...  27.1 us
    psum x1, blocking collectives, local(): lax.psum((jnp.sum(scaled_cot, axis=1), jnp.sum(scaled_cot * normalized, a...  21.9 us
    ppermute x1, waiting for transfers between devices, passed_along(): lax.ppermute(array, axis, [(i, (i + by) % length) for i in range(length)])  5.69 us
    reduce_sum x1, other arithmetic, local(): summed = jnp.sum(parts, axis=0)  5.39 us
    ppermute x1, starting transfers between devices, passed_along(): lax.ppermute(array, axis, [(i, (i + by) % length) for i in range(length)])  5.37 us
    ppermute x1, starting transfers between devices, shifted(): lax.ppermute(value, axis, [(source, source + steps) for source in range(l...  4.82 us
  transfers between devices with their start and end apart: 3, of which 3 were waited for; matrix products, arithmetic and copies ran while one was open for 2% of the time, Pallas kernels for 0%

profile of v1, /device:TPU:1, one launch (start us, length us, event | category | flops | bytes accessed | tf_op | source)
XLA Modules:
  0.0 210.9 jit_solution(11721272389914477621)
XLA Ops:
  7.2 0.0 copy-start
  7.2 0.0 all-gather.3.cloned.1.call-start
  7.2 4.8 %collective-permute-start = (bf16[1,128,1536]{2,1,0:T(8,128)(2,1)}, bf16[1,128,1536]{2,1,0:T(8,128)(2,1)}, u32[]{:S(2)}, u32[]{:S(2)}) collective-permute-start(bf16[1,128,1536]{2,1,0:T(8,128)(2,1)} %param.10), channel_id=1, source_target_pairs={{0,8},{8,16},{16,24},{1,9},{9,17},{17,25},{2,10},{10,18},{18,26},{... | collective-permute-start | bytes 1179656 | tf_op jit(solution)/shard_map/ppermute | solution.py:14
  12.0 0.7 select_reduce_fusion
  12.8 0.0 copy-done
  12.8 0.6 gather_fusion.1
  13.4 1.6 gather_fusion
  15.0 0.0 copy-start.1
  15.0 0.1 broadcast_select_fusion.1
  15.1 0.0 copy-start.2
  15.2 0.0 copy-start.4
  15.2 0.1 bitcast_convert_fusion
  15.3 1.1 collective-permute-done
  16.3 0.0 copy-done.1
  16.3 1.2 convert_reduce_fusion
  17.6 27.1 %all-reduce.1 = (f32[128]{0:T(128)S(1)}, f32[128]{0:T(128)S(1)}) all-reduce(f32[128]{0:T(128)S(1)} %get-tuple-element.8, f32[128]{0:T(128)S(1)} %get-tuple-element.7), channel_id=1, replica_groups=mesh['dp'=16,'pipe'=4,'tensor'=8] {'tensor'}, use_global_device_ids=true, to_apply=%region_3.4 | all-reduce | flops 256 | bytes 2048 | tf_op jit(solution)/shard_map/psum | solution.py:48
  44.7 0.0 copy-done.2
  44.7 0.0 copy-done.4
  44.7 0.5 fusion.17
  45.2 0.0 copy-start.5
  45.2 1.7 fusion.2
  46.9 0.0 all-gather.3.cloned.1.call-update
  46.9 0.0 copy-done.5
  46.9 21.9 %all-reduce = (f32[128]{0:T(128)S(1)}, f32[128]{0:T(128)S(1)}) all-reduce(f32[128]{0:T(128)S(1)} %get-tuple-element.6, f32[128]{0:T(128)S(1)} %get-tuple-element.5), channel_id=1, replica_groups=mesh['dp'=16,'pipe'=4,'tensor'=8] {'tensor'}, use_global_device_ids=true, to_apply=%region_8.10 | all-reduce | flops 256 | bytes 2048 | tf_op jit(solution)/shard_map/psum | solution.py:55
  68.9 0.0 copy-start.3
  68.9 0.4 fusion.15
  69.2 0.6 gather_fusion.2
  69.8 0.1 broadcast_select_fusion
  69.9 5.4 %collective-permute-start.1 = (bf16[1,128,1536]{2,1,0:T(8,128)(2,1)S(1)}, bf16[1,128,1536]{2,1,0:T(8,128)(2,1)S(1)}, u32[]{:S(2)}, u32[]{:S(2)}) collective-permute-start(bf16[1,128,1536]{2,1,0:T(8,128)(2,1)S(1)} %bitcast.44), channel_id=1, source_target_pairs={{0,24},{8,0},{16,8},{24,16},{1,25},{9,1},{17,9},{25,17},{2,26},{10... | collective-permute-start | bytes 1179656 | tf_op jit(solution)/shard_map/ppermute | solution.py:19
  75.3 0.0 copy-done.3
  75.3 1.1 fusion.1
  76.4 5.7 %collective-permute-done.1 = bf16[1,128,1536]{2,1,0:T(8,128)(2,1)S(1)} collective-permute-done((bf16[1,128,1536]{2,1,0:T(8,128)(2,1)S(1)}, bf16[1,128,1536]{2,1,0:T(8,128)(2,1)S(1)}, u32[]{:S(2)}, u32[]{:S(2)}) %collective-permute-start.1) | collective-permute-done | bytes 393248 | tf_op jit(solution)/shard_map/ppermute | solution.py:19
  82.0 114.9 %all-gather.3.cloned.1.call-done = f32[1024,3072]{1,0:T(8,128)} async-done(((f32[64,3072]{1,0:T(8,128)}), f32[1024,3072]{1,0:T(8,128)}) %all-gather.3.cloned.1.call-update) | async-done | bytes 12582928 | tf_op jit(solution)/shard_map/all_gather | solution.py:73
  196.9 5.4 %reduce_sum.59 = f32[64,3072]{1,0:T(8,128)S(1)} reduce(f32[16,64,3072]{2,1,0:T(8,128)} %bitcast.41, f32[]{:T(128)} %constant.25.clone.1), dimensions={0}, to_apply=%region_9.11 | reduce | flops 2949120 | bytes 13369348 | tf_op jit(solution)/shard_map/reduce_sum | solution.py:74
  202.3 0.9 slice_bitcast_fusion
  203.3 0.7 copy.13
  (8 shorter events, 0.1 us)
Async XLA Ops:
  7.2 5.7 %copy-start = (bf16[1,128,1536]{2,1,0:T(8,128)(2,1)S(1)}, bf16[1,128,1536]{2,1,0:T(8,128)(2,1)}, u32[]{:S(2)}) copy-start(bf16[1,128,1536]{2,1,0:T(8,128)(2,1)} %param.12) | copy-start | bytes 1179652
  7.2 189.8 %all-gather.3.cloned.1.call-start = ((), (), s32[]{:S(2)}) async-start(), calls=%async_computation | async-start | bytes 13369344 | tf_op jit(solution)/shard_map/all_gather | solution.py:73
  7.2 9.1 %collective-permute-start = (bf16[1,128,1536]{2,1,0:T(8,128)(2,1)}, bf16[1,128,1536]{2,1,0:T(8,128)(2,1)}, u32[]{:S(2)}, u32[]{:S(2)}) collective-permute-start(bf16[1,128,1536]{2,1,0:T(8,128)(2,1)} %param.10), channel_id=1, source_target_pairs={{0,8},{8,16},{16,24},{1,9},{9,17},{17,25},{2,10},{10,18},{18,26},{... | collective-permute-start | bytes 1179656 | tf_op jit(solution)/shard_map/ppermute | solution.py:14
  15.0 1.3 copy-start.1
  15.1 29.5 %copy-start.2 = (bf16[1,64,1536]{2,1,0:T(8,128)(2,1)S(1)}, bf16[1,64,1536]{2,1,0:T(8,128)(2,1)}, u32[]{:S(2)}) copy-start(bf16[1,64,1536]{2,1,0:T(8,128)(2,1)} %param.14) | copy-start | bytes 589828
  15.2 29.5 %copy-start.4 = (s32[128]{0:T(128)S(1)}, s32[128]{0:T(128)}, u32[]{:S(2)}) copy-start(s32[128]{0:T(128)} %param.16) | copy-start | bytes 1540
  45.2 1.7 copy-start.5
  68.9 6.4 %copy-start.3 = (bf16[1,64,1536]{2,1,0:T(8,128)(2,1)S(1)}, bf16[1,64,1536]{2,1,0:T(8,128)(2,1)}, u32[]{:S(2)}) copy-start(bf16[1,64,1536]{2,1,0:T(8,128)(2,1)} %param.15) | copy-start | bytes 589828
  69.9 12.1 %collective-permute-start.1 = (bf16[1,128,1536]{2,1,0:T(8,128)(2,1)S(1)}, bf16[1,128,1536]{2,1,0:T(8,128)(2,1)S(1)}, u32[]{:S(2)}, u32[]{:S(2)}) collective-permute-start(bf16[1,128,1536]{2,1,0:T(8,128)(2,1)S(1)} %bitcast.44), channel_id=1, source_target_pairs={{0,24},{8,0},{16,8},{24,16},{1,25},{9,1},{17,9},{25,17},{2,26},{10... | collective-permute-start | bytes 1179656 | tf_op jit(solution)/shard_map/ppermute | solution.py:19
Sparse Core Ops, SparseCore 0:
  47.0 149.8 all-gather.2
